TPU v7x, 32 devices: a whole 2x2x4 slice. The times are simulated.
32 devices in a mesh: group: 2 (over x), slab: 16 (over z, y, core).
Axes of the slice: x: 2, y: 2, z: 4, core: 2. Of those that a mesh axis runs over, the one named last changes fastest.
Arguments:
- queries: bfloat16 [16384, 512], P(('group', 'slab')), may hold values from -6 to 6
- keys: bfloat16 [16384, 512], P(('group', 'slab')), may hold values from -6 to 6
- values: bfloat16 [16384, 512], P(('group', 'slab')), may hold values from -6 to 6
- neighbours: int32 [128, 6], P(('group', 'slab')), may hold values from 0 to 15, as said below
- live_tiles: int32 [32], P(('group', 'slab')), may hold values from 1 to 4, as said below
- boundary_ids: int32 [32, 4], P(('group', 'slab')), may hold values from 0 to 3, as said below
Outputs:
- attended: bfloat16 [16384, 512], P(('group', 'slab'))
Inputs may be any that keep to these rules, and one draw needn't show every extreme that they name: `neighbours`: each row names 6 different positions of the pool. `live_tiles`: some slab has all 4 tiles active. `boundary_ids`: each row names 4 different tiles of its slab.
All inputs are finite; a program needn't handle non-finite values.
Results may differ from a plain program's by a relative error of at most 0.008.
Values may be sent and summed in bfloat16 or wider, within the bound.
A program may use at most 128 MiB of HBM per device.

v0:
```python
import jax
import jax.numpy as jnp
from jax import lax
from jax.sharding import PartitionSpec as P

HEADS = 8
HEAD_DIM = 64
TILE = 128
HALO = 4
BLOCK = 4


def shifted(block, axis, distance):
    devices = range(lax.axis_size(axis))
    route = [((i - distance) % len(devices), i) for i in devices]
    return lax.ppermute(block, axis, route)


def attend_block(number, tile_queries, pool, lists, live):
    width = tile_queries.shape[2]
    tile = tile_queries.shape[1]
    start = number * BLOCK
    listed = lists.shape[1]
    key_set = pool[0][lists].reshape(BLOCK, listed * tile, HEADS, HEAD_DIM)
    value_set = pool[1][lists].reshape(BLOCK, listed * tile, HEADS, HEAD_DIM)
    query_set = tile_queries.reshape(BLOCK, tile, HEADS, HEAD_DIM)
    scores = jnp.einsum(
        "qihd,qjhd->qhij", query_set, key_set, preferred_element_type=jnp.float32
    ) * HEAD_DIM ** (-0.5)
    weights = jax.nn.softmax(scores, axis=-1).astype(jnp.bfloat16)
    mixed = jnp.einsum("qhij,qjhd->qihd", weights, value_set, preferred_element_type=jnp.float32)
    alive = start + jnp.arange(BLOCK, dtype=jnp.int32) < live
    mixed = jnp.where(alive[:, None, None, None], mixed, 0.0)
    return mixed.astype(jnp.bfloat16).reshape(BLOCK, tile, width)


def shards(queries, keys, values, neighbours, live_tiles, boundary_ids):
    tile = TILE
    count = queries.shape[0] // tile
    width = queries.shape[1]
    pairs = jnp.stack([keys, values])
    before = shifted(pairs, "slab", 1)
    after = shifted(pairs, "slab", -1)
    tiled = pairs.reshape(2, count, tile, width)
    remote, remote_ids = shifted((tiled, boundary_ids), "group", 1)
    border = remote[:, remote_ids[0]]
    pool = jnp.concatenate(
        [tiled, before.reshape(2, HALO, tile, width), after.reshape(2, HALO, tile, width), border],
        axis=1,
    )
    tile_queries = queries.reshape(count, tile, width)
    live = live_tiles[0]
    blocks = count // BLOCK
    outputs = lax.map(
        lambda number: attend_block(number, tile_queries, pool, neighbours, live),
        jnp.arange(blocks, dtype=jnp.int32),
    )
    result = outputs.reshape(count * tile, width)
    return result


def solution(mesh):
    in_specs = (
        P(("group", "slab"), None),
        P(("group", "slab"), None),
        P(("group", "slab"), None),
        P(("group", "slab"), None),
        P(("group", "slab")),
        P(("group", "slab"), None),
    )
    out_specs = P(("group", "slab"), None)
    return jax.shard_map(shards, mesh=mesh, in_specs=in_specs, out_specs=out_specs, check_vma=False)
```

profile of v0, /device:TPU:1, one launch (start us, length us, event | category | flops | bytes accessed | tf_op | source)
XLA Modules:
  0.0 99.7 jit_solution(10675719755949984914)
XLA Ops:
  0.0 0.0 copy-start.1
  0.0 0.0 copy-start
  0.0 1.4 %pad_maximum_fusion.1 = bf16[2,4,128,512]{3,2,0,1:T(8,128)(2,1)S(1)} fusion(bf16[1,4,128,512]{3,2,0,1:T(8,128)(2,1)} %bitcast.40, bf16[1,4,128,512]{3,2,0,1:T(8,128)(2,1)} %bitcast.43), kind=kLoop, calls=%fused_computation.21 | loop fusion | flops 524288 | bytes 2097152 | tf_op jit(solution)/shard_map/stack | solution.py:41
  1.4 2.1 %collective-permute-start.2 = (bf16[2,4,128,512]{3,2,0,1:T(8,128)(2,1)S(1)}, bf16[2,4,128,512]{3,2,0,1:T(8,128)(2,1)}, u32[]{:S(2)}, u32[]{:S(2)}) collective-permute-start(bf16[2,4,128,512]{3,2,0,1:T(8,128)(2,1)S(1)} %pad_maximum_fusion.1), channel_id=1, source_target_pairs={{16,0},{0,16},{17,1},{1,17},{18,2},{2,18},{19,3},{3,19},{20,4},{4,... | collective-permute-start | bytes 3145736 | tf_op jit(solution)/shard_map/ppermute | solution.py:16
  3.5 2.3 %pad_maximum_fusion.2 = bf16[2,512,512]{2,1,0:T(8,128)(2,1)} fusion(bf16[1,512,512]{2,1,0:T(8,128)(2,1)} %bitcast.41, bf16[1,512,512]{2,1,0:T(8,128)(2,1)} %bitcast.44), kind=kLoop, calls=%fused_computation.22 | loop fusion | flops 524288 | bytes 2097152 | tf_op jit(solution)/shard_map/stack | solution.py:41
  5.8 2.1 %collective-permute-start = (bf16[2,512,512]{2,1,0:T(8,128)(2,1)}, bf16[2,512,512]{2,1,0:T(8,128)(2,1)}, u32[]{:S(2)}, u32[]{:S(2)}) collective-permute-start(bf16[2,512,512]{2,1,0:T(8,128)(2,1)} %pad_maximum_fusion.2), channel_id=1, source_target_pairs={{15,0},{0,1},{1,2},{2,3},{3,4},{4,5},{5,6},{6,7},{7,8},{8,9},{9,10... | collective-permute-start | bytes 3145736 | tf_op jit(solution)/shard_map/ppermute | solution.py:16
  7.9 0.0 collective-permute-start.1
  7.9 0.3 collective-permute-start.3
  8.1 0.7 compare_select_fusion
  8.8 0.1 reshape.75
  8.9 1.6 %reshape.97 = bf16[4,128,8,64]{3,2,1,0:T(8,128)(2,1)S(1)} reshape(bf16[512,512]{1,0:T(8,128)(2,1)} %param.6) | data formatting | bytes 1048576 | tf_op jit(solution)/shard_map/while/body/eval_jaxpr/reshape;reshape | solution.py:26
  11.2 15.3 %collective-permute-done.3 = s32[1,4]{1,0:T(1,128)S(1)} collective-permute-done((s32[1,4]{1,0:T(1,128)}, s32[1,4]{1,0:T(1,128)S(1)}, u32[]{:S(2)}, u32[]{:S(2)}) %collective-permute-start.3) | collective-permute-done | bytes 48 | tf_op jit(solution)/shard_map/ppermute | solution.py:16
  26.5 0.0 collective-permute-done.2
  26.5 1.3 %copy.19 = bf16[2,4,128,512]{3,2,1,0:T(8,128)(2,1)S(1)} copy(bf16[2,4,128,512]{3,2,0,1:T(8,128)(2,1)} %collective-permute-done.2) | data formatting | bytes 2097152 | tf_op jit(solution)/shard_map/ppermute | solution.py:16
  27.8 1.6 %gather_fusion = bf16[4,2,128,512]{3,2,1,0:T(8,128)(2,1)} fusion(bf16[2,4,128,512]{3,2,1,0:T(8,128)(2,1)S(1)} %copy.19, s32[1024]{0:T(1024)S(1)} %pad_clamp_fusion.1), kind=kCustom, calls=%fused_computation | custom fusion | bytes 2097168 | tf_op jit(solution)/shard_map/gather | solution.py:46
  29.4 1.7 %collective-permute-done = bf16[2,512,512]{2,1,0:T(8,128)(2,1)} collective-permute-done((bf16[2,512,512]{2,1,0:T(8,128)(2,1)}, bf16[2,512,512]{2,1,0:T(8,128)(2,1)}, u32[]{:S(2)}, u32[]{:S(2)}) %collective-permute-start) | collective-permute-done | bytes 1048608 | tf_op jit(solution)/shard_map/ppermute | solution.py:16
  31.2 2.5 %collective-permute-done.1 = bf16[2,512,512]{2,1,0:T(8,128)(2,1)} collective-permute-done((bf16[2,512,512]{2,1,0:T(8,128)(2,1)}, bf16[2,512,512]{2,1,0:T(8,128)(2,1)}, u32[]{:S(2)}, u32[]{:S(2)}) %collective-permute-start.1) | collective-permute-done | bytes 1048608 | tf_op jit(solution)/shard_map/ppermute | solution.py:16
  33.6 0.0 copy-done.1
  33.6 0.0 copy-done
  33.6 2.0 %pad_maximum_fusion = bf16[2,16,128,512]{3,2,0,1:T(8,128)(2,1)S(1)} fusion(bf16[2,4,128,512]{3,2,0,1:T(8,128)(2,1)} %bitcast.46, bf16[1,4,128,512]{3,2,0,1:T(8,128)(2,1)S(1)} %bitcast.42, bf16[1,4,128,512]{3,2,0,1:T(8,128)(2,1)S(1)} %bitcast.45, bf16[2,4,128,512]{3,2,1,0:T(8,128)(2,1)} %bitcast.5, bf16[2,4,128,512]{3,2,1,0:T(8,128)(2,1)} %bitcast.6), kind=kLoop, calls=%fused_computation.15 | loop fusion | flops 20971520 | bytes 8388608 | tf_op jit(solution)/shard_map/concatenate | solution.py:47
  35.7 1.6 %slice_bitcast_fusion.1 = (bf16[16,128,512]{2,1,0:T(8,128)(2,1)S(1)}, bf16[16,128,512]{2,1,0:T(8,128)(2,1)}) fusion(bf16[2,16,128,512]{3,2,0,1:T(8,128)(2,1)S(1)} %pad_maximum_fusion), kind=kLoop, calls=%fused_computation.17 | loop fusion | bytes 8388608 | tf_op jit(solution)/shard_map/while/body/eval_jaxpr/squeeze | solution.py:25
  37.3 4.1 %gather_fusion.2 = bf16[24,128,512]{2,1,0:T(8,128)(2,1)} fusion(bf16[16,128,512]{2,1,0:T(8,128)(2,1)} %get-tuple-element.16, s32[1024]{0:T(1024)S(1)} %pad_clamp_fusion), kind=kCustom, calls=%fused_computation.2 | custom fusion | bytes 6291552 | tf_op jit(solution)/shard_map/while/body/eval_jaxpr/gather | solution.py:24
  41.4 8.9 %reshape.96 = bf16[4,768,8,64]{3,2,1,0:T(8,128)(2,1)} reshape(bf16[24,128,512]{2,1,0:T(8,128)(2,1)} %gather_fusion.2) | data formatting | bytes 6291456 | tf_op jit(solution)/shard_map/while/body/eval_jaxpr/reshape | solution.py:24
  50.4 9.2 %fusion.6 = f32[4,8,768,128]{3,2,1,0:T(8,128)} fusion(bf16[4,768,8,64]{3,2,1,0:T(8,128)(2,1)} %reshape.96, bf16[4,128,8,64]{3,2,1,0:T(8,128)(2,1)S(1)} %reshape.97), kind=kOutput, calls=%fused_computation.10 | convolution fusion | flops 402653184 | bytes 16252928 | tf_op jit(solution)/shard_map/while/body/eval_jaxpr/qihd,qjhd->qhij/dot_general | solution.py:27
  59.5 11.1 %fusion.30 = f32[4,8,128]{2,1,0:T(8,128)S(1)} fusion(f32[4,8,768,128]{3,2,1,0:T(8,128)} %fusion.6), kind=kOutput, calls=%fused_computation.33 | output fusion | flops 12583679 | bytes 12599296 | tf_op jit(solution)/shard_map/while/body/eval_jaxpr/sub | solution.py:30
  70.6 2.5 %gather_fusion.1 = bf16[24,128,512]{2,1,0:T(8,128)(2,1)} fusion(bf16[16,128,512]{2,1,0:T(8,128)(2,1)S(1)} %get-tuple-element.15, s32[1024]{0:T(1024)S(1)} %pad_clamp_fusion), kind=kCustom, calls=%fused_computation.1 | custom fusion | bytes 6291552 | tf_op jit(solution)/shard_map/while/body/eval_jaxpr/gather | solution.py:25
  73.2 8.9 %reshape.95 = bf16[4,768,8,64]{3,2,1,0:T(8,128)(2,1)} reshape(bf16[24,128,512]{2,1,0:T(8,128)(2,1)} %gather_fusion.1) | data formatting | bytes 6291456 | tf_op jit(solution)/shard_map/while/body/eval_jaxpr/reshape | solution.py:25
  82.1 15.6 %fusion.17 = bf16[4,128,8,64]{1,3,2,0:T(8,128)(2,1)S(1)} fusion(f32[4,8,128]{2,1,0:T(8,128)S(1)} %fusion.30, bf16[4,768,8,64]{3,2,1,0:T(8,128)(2,1)} %reshape.95, pred[4]{0:T(512)(128)(4,1)S(1)} %iota_compare_fusion, f32[4,8,768,128]{3,2,1,0:T(8,128)} %fusion.6), kind=kOutput, calls=%fused_computation.20 | convolution fusion | flops 418910976 | bytes 16269316 | tf_op jit(solution)/shard_map/while/body/eval_jaxpr/qhij,qjhd->qihd/dot_general | solution.py:31
  97.7 0.6 copy.38
  98.2 1.4 %reshape.98 = bf16[512,512]{1,0:T(8,128)(2,1)} reshape(bf16[4,128,8,64]{3,2,1,0:T(8,128)(2,1)S(1)} %copy.38) | data formatting | bytes 1048576 | tf_op jit(solution)/shard_map/reshape | solution.py:58
  (4 shorter events, 0.0 us)
Async XLA Ops:
  0.0 33.6 %copy-start.1 = (bf16[512,512]{1,0:T(8,128)(2,1)S(1)}, bf16[512,512]{1,0:T(8,128)(2,1)}, u32[]{:S(2)}) copy-start(bf16[512,512]{1,0:T(8,128)(2,1)} %param.7) | copy-start | bytes 1572868
  0.0 33.6 %copy-start = (bf16[512,512]{1,0:T(8,128)(2,1)S(1)}, bf16[512,512]{1,0:T(8,128)(2,1)}, u32[]{:S(2)}) copy-start(bf16[512,512]{1,0:T(8,128)(2,1)} %param.8) | copy-start | bytes 1572868
  1.4 25.1 %collective-permute-start.2 = (bf16[2,4,128,512]{3,2,0,1:T(8,128)(2,1)S(1)}, bf16[2,4,128,512]{3,2,0,1:T(8,128)(2,1)}, u32[]{:S(2)}, u32[]{:S(2)}) collective-permute-start(bf16[2,4,128,512]{3,2,0,1:T(8,128)(2,1)S(1)} %pad_maximum_fusion.1), channel_id=1, source_target_pairs={{16,0},{0,16},{17,1},{1,17},{18,2},{2,18},{19,3},{3,19},{20,4},{4,... | collective-permute-start | bytes 3145736 | tf_op jit(solution)/shard_map/ppermute | solution.py:16
  5.8 25.4 %collective-permute-start = (bf16[2,512,512]{2,1,0:T(8,128)(2,1)}, bf16[2,512,512]{2,1,0:T(8,128)(2,1)}, u32[]{:S(2)}, u32[]{:S(2)}) collective-permute-start(bf16[2,512,512]{2,1,0:T(8,128)(2,1)} %pad_maximum_fusion.2), channel_id=1, source_target_pairs={{15,0},{0,1},{1,2},{2,3},{3,4},{4,5},{5,6},{6,7},{7,8},{8,9},{9,10... | collective-permute-start | bytes 3145736 | tf_op jit(solution)/shard_map/ppermute | solution.py:16
  7.9 25.8 %collective-permute-start.1 = (bf16[2,512,512]{2,1,0:T(8,128)(2,1)}, bf16[2,512,512]{2,1,0:T(8,128)(2,1)}, u32[]{:S(2)}, u32[]{:S(2)}) collective-permute-start(bf16[2,512,512]{2,1,0:T(8,128)(2,1)} %pad_maximum_fusion.2), channel_id=1, source_target_pairs={{1,0},{2,1},{3,2},{4,3},{5,4},{6,5},{7,6},{8,7},{9,8},{10,9},{11,1... | collective-permute-start | bytes 3145736 | tf_op jit(solution)/shard_map/ppermute | solution.py:16
  7.9 18.6 %collective-permute-start.3 = (s32[1,4]{1,0:T(1,128)}, s32[1,4]{1,0:T(1,128)S(1)}, u32[]{:S(2)}, u32[]{:S(2)}) collective-permute-start(s32[1,4]{1,0:T(1,128)} %param.11), channel_id=1, source_target_pairs={{16,0},{0,16},{17,1},{1,17},{18,2},{2,18},{19,3},{3,19},{20,4},{4,... | collective-permute-start | bytes 56 | tf_op jit(solution)/shard_map/ppermute | solution.py:16
where the time goes:
time: 100 us; the launch traced here: 99.7 us
  local copies, waits for them, and re-layouts  32.7 us (33%)
  matrix products  24.8 us (25%)
  waiting for transfers between devices  19.5 us (20%)
  other arithmetic  17.5 us (18%)
  starting transfers between devices  4.43 us (4%)
    ppermute x4, waiting for transfers between devices, shifted(): return lax.ppermute(block, axis, route)  19.5 us
    dot_general x1, matrix products, attend_block(): jnp.einsum('qhij,qjhd->qihd', weights, value_set, preferred_element_type=...  15.6 us
    sub x1, other arithmetic, attend_block(): weights = jax.nn.softmax(scores, axis=-1).astype(jnp.bfloat16)  11.1 us
    dot_general x1, matrix products, attend_block(): jnp.einsum('qihd,qjhd->qhij', query_set, key_set, preferred_element_type=...  9.15 us
    reshape x1, local copies, waits for them, and re-layouts, attend_block(): value_set = pool[1][lists].reshape(BLOCK, listed * tile, HEADS, HEAD_DIM)  8.92 us
    reshape x1, local copies, waits for them, and re-layouts, attend_block(): key_set = pool[0][lists].reshape(BLOCK, listed * tile, HEADS, HEAD_DIM)  8.91 us
    ppermute x4, starting transfers between devices, shifted(): return lax.ppermute(block, axis, route)  4.43 us
    gather x1, local copies, waits for them, and re-layouts, attend_block(): key_set = pool[0][lists].reshape(BLOCK, listed * tile, HEADS, HEAD_DIM)  4.11 us
  transfers between devices with their start and end apart: 4, of which 3 were waited for; matrix products, arithmetic and copies ran while one was open for 8% of the time, Pallas kernels for 0%

commit v1 on v0

v1 whole, which is shorter than its diff:
```python
import functools
import math

import jax
import jax.numpy as jnp
from jax import lax
from jax.experimental import pallas as pl
from jax.experimental.pallas import tpu as pltpu
from jax.sharding import PartitionSpec as P

HEAD_DIM = 64
TILE = 128
NEVER = -1e38
LOWEST = -1e30
SCALE = HEAD_DIM ** (-0.5) * math.log2(math.e)
NT = (((1,), (1,)), ((), ()))
NN = (((1,), (0,)), ((), ()))


def dot(a, b, dims):
    return lax.dot_general(a, b, dims, preferred_element_type=jnp.float32)


def kernel(
    groups, slabs,
    q_ref, k_ref, v_ref, lists_ref, live_ref, ids_ref,
    out_ref,
    pool_k, pool_v, q_raw, q_pairs, acc, top, bias, far_ids,
    local_sem, send_sem, recv_sem, ids_sem,
):
    count = lists_ref.shape[0]
    listed = lists_ref.shape[1]
    pairs = q_pairs.shape[0]
    wide = 2 * HEAD_DIM
    group = lax.axis_index("group")
    slab = lax.axis_index("slab")
    odd = lax.rem(slab, 2)
    near = slab + 1 - 2 * odd
    far = lax.rem(slab - 1 + 2 * odd + slabs, slabs)
    ahead = lax.rem(group + 1, groups)
    behind = lax.rem(group - 1 + groups, groups)
    at_near = {"group": group, "slab": near}
    at_far = {"group": group, "slab": far}
    at_ahead = {"group": ahead, "slab": slab}
    at_behind = {"group": behind, "slab": slab}
    mesh_id = pl.DeviceIdType.MESH

    barrier = pltpu.get_barrier_semaphore()
    for device in (at_near, at_far, at_behind):
        pl.semaphore_signal(barrier, inc=1, device_id=device, device_id_type=mesh_id)

    def slot(place, number):
        if place < 2:
            return (place * count + number) // 2, lax.rem(place * count + number, 2)
        return count + number, place - 2

    def rows(place, number):
        chunk, half = slot(place, number)
        return chunk, pl.ds(half * TILE, TILE)

    def piece(ref, number):
        return ref.at[pl.ds(number * TILE, TILE)]

    def own(number, kind):
        ref, pool = ((k_ref, pool_k), (v_ref, pool_v))[kind]
        chunk, at = rows(0, number)
        return pltpu.make_async_copy(piece(ref, number), pool.at[chunk, at], local_sem.at[kind, number])

    def remote(place, number, kind):
        ref, pool = ((k_ref, pool_k), (v_ref, pool_v))[kind]
        chunk, at = rows(place, number)
        return pltpu.make_async_remote_copy(
            src_ref=piece(ref, number),
            dst_ref=pool.at[chunk, at],
            send_sem=send_sem.at[place - 1, kind, number],
            recv_sem=recv_sem.at[place - 1, kind, number],
            device_id=(at_near, at_far, at_ahead)[place - 1],
            device_id_type=mesh_id,
        )

    q_copy = pltpu.make_async_copy(q_ref, q_raw, local_sem.at[2, 0])
    q_copy.start()
    for number in range(count):
        for kind in range(2):
            own(number, kind).start()

    ids_copy = pltpu.make_async_remote_copy(
        src_ref=ids_ref, dst_ref=far_ids, send_sem=ids_sem.at[0], recv_sem=ids_sem.at[1],
        device_id=at_ahead, device_id_type=mesh_id,
    )
    pl.semaphore_wait(barrier, 3)
    ids_copy.start()
    for number in range(count):
        for place in (3, 2, 1):
            for kind in range(2):
                remote(place, number, kind).start()

    def listing(tile, position):
        hit = lists_ref[tile, 0] == position
        for entry in range(1, listed):
            hit = jnp.logical_or(hit, lists_ref[tile, entry] == position)
        return jnp.where(hit, 0.0, NEVER).astype(jnp.float32)

    near_at = 2 * count - odd * count
    far_at = count + odd * count
    for tile in range(count):
        for number in range(count):
            for place, first in ((0, 0), (1, near_at), (2, far_at)):
                chunk, half = slot(place, number)
                bias[tile, chunk, pl.ds(half, 1)] = jnp.full((1, 2 * TILE), listing(tile, first + number))

    q_copy.wait()
    low = lax.broadcasted_iota(jnp.int32, (TILE, wide), 1) < HEAD_DIM
    for pair in range(pairs):
        for tile in range(count):
            block = q_raw[pl.ds(tile * TILE, TILE), pl.ds(pair * wide, wide)]
            zero = jnp.zeros_like(block)
            q_pairs[pair, tile, pl.ds(0, TILE)] = jnp.where(low, block, zero)
            q_pairs[pair, tile, pl.ds(TILE, TILE)] = jnp.where(low, zero, block)
    acc[...] = jnp.zeros_like(acc)
    top[...] = jnp.full(top.shape, LOWEST, jnp.float32)

    ones = jnp.ones((16, 2 * TILE), jnp.bfloat16)

    def update(chunk, pair, tile, values):
        keys = pool_k[chunk, :, pl.ds(pl.multiple_of(pair * wide, wide), wide)]
        scores = dot(keys, q_pairs[pair, tile], NT)
        first, second = scores[:TILE], scores[TILE:]
        first_bias, second_bias = bias[tile, chunk, 0:1], bias[tile, chunk, 1:2]
        before = top[pair, tile, 0:1]
        after = jnp.maximum(
            before,
            jnp.maximum(
                jnp.max(first, axis=0, keepdims=True) + first_bias,
                jnp.max(second, axis=0, keepdims=True) + second_bias,
            ),
        )
        shrink = jnp.exp2((before - after) * SCALE)
        weights = jnp.concatenate(
            [
                jnp.exp2((first - (after - first_bias)) * SCALE).astype(jnp.bfloat16),
                jnp.exp2((second - (after - second_bias)) * SCALE).astype(jnp.bfloat16),
            ],
            axis=0,
        )
        mixed = dot(values, weights, NN)
        upper = acc[pair, tile, :HEAD_DIM] * shrink + jnp.concatenate(
            [mixed[:HEAD_DIM, :TILE], mixed[HEAD_DIM:wide, TILE:]], axis=1
        )
        total = acc[pair, tile, HEAD_DIM:] * shrink + mixed[wide:wide + 8]
        return after, upper, total

    def chunk_values(chunk, pair):
        block = pool_v[chunk, :, pl.ds(pl.multiple_of(pair * wide, wide), wide)]
        return jnp.concatenate([block.T, ones], axis=0)

    def run(chunk):
        def one_pair(pair, carry):
            values = chunk_values(chunk, pair)
            for tile in range(count):
                after, upper, total = update(chunk, pair, tile, values)
                top[pair, tile, 0:1] = after
                acc[pair, tile, :HEAD_DIM] = upper
                acc[pair, tile, HEAD_DIM:] = total
            return carry

        lax.fori_loop(0, pairs, one_pair, 0)

    for number in range(count):
        for kind in range(2):
            own(number, kind).wait()
    lax.fori_loop(0, count // 2, lambda i, c: (run(i), c)[1], 0)
    for number in range(count):
        for kind in range(2):
            remote(1, number, kind).wait()
    lax.fori_loop(count // 2, count, lambda i, c: (run(i), c)[1], 0)

    ids_copy.wait()
    for tile in range(count):
        given = [listing(tile, 3 * count + entry) for entry in range(count)]
        for number in range(count):
            row = jnp.full((1, 2 * TILE), NEVER, jnp.float32)
            for entry in range(count):
                hit = jnp.broadcast_to(far_ids[0:1, entry:entry + 1], (1, 2 * TILE)) == number
                row = jnp.where(hit, given[entry], row)
            bias[tile, count + number, 1:2] = row

    def later(number, carry):
        for place in (2, 3):
            for kind in range(2):
                remote(place, number, kind).wait()
        run(count + number)
        return carry

    lax.fori_loop(0, count - 1, later, 0)
    for place in (2, 3):
        for kind in range(2):
            remote(place, count - 1, kind).wait()

    live = live_ref[0]

    def last(pair, carry):
        chunk = 2 * count - 1
        values = chunk_values(chunk, pair)
        for tile in range(count):
            _, upper, total = update(chunk, pair, tile, values)
            mixed = upper / total[0:1]
            mixed = jnp.concatenate([mixed[:, :TILE], mixed[:, TILE:]], axis=0)
            mixed = jnp.where(tile < live, mixed.T, 0.0)
            at = pl.ds(pl.multiple_of(pair * wide, wide), wide)
            out_ref[pl.ds(tile * TILE, TILE), at] = mixed.astype(out_ref.dtype)
        return carry

    lax.fori_loop(0, pairs, last, 0)


def solution(mesh):
    groups, slabs = mesh.shape["group"], mesh.shape["slab"]

    def shards(queries, keys, values, neighbours, live_tiles, boundary_ids):
        nodes, width = queries.shape
        count = neighbours.shape[0]
        pairs = width // (2 * HEAD_DIM)
        anywhere = pl.BlockSpec(memory_space=pl.ANY)
        scalars = pl.BlockSpec(memory_space=pltpu.SMEM)
        inside = pl.BlockSpec(memory_space=pltpu.VMEM)
        return pl.pallas_call(
            functools.partial(kernel, groups, slabs),
            out_shape=jax.ShapeDtypeStruct((nodes, width), queries.dtype),
            in_specs=[anywhere, anywhere, anywhere, scalars, scalars, inside],
            out_specs=inside,
            scratch_shapes=[
                pltpu.VMEM((2 * count, 2 * TILE, width), keys.dtype),
                pltpu.VMEM((2 * count, 2 * TILE, width), values.dtype),
                pltpu.VMEM((nodes, width), queries.dtype),
                pltpu.VMEM((pairs, count, 2 * TILE, 2 * HEAD_DIM), queries.dtype),
                pltpu.VMEM((pairs, count, HEAD_DIM + 8, 2 * TILE), jnp.float32),
                pltpu.VMEM((pairs, count, 8, 2 * TILE), jnp.float32),
                pltpu.VMEM((count, 2 * count, 2, 2 * TILE), jnp.float32),
                pltpu.VMEM(boundary_ids.shape, jnp.int32),
                pltpu.SemaphoreType.DMA((3, count)),
                pltpu.SemaphoreType.DMA((3, 2, count)),
                pltpu.SemaphoreType.DMA((3, 2, count)),
                pltpu.SemaphoreType.DMA((2,)),
            ],
            compiler_params=pltpu.CompilerParams(collective_id=0, has_side_effects=True),
        )(queries, keys, values, neighbours, live_tiles, boundary_ids)

    rows = P(("group", "slab"), None)
    return jax.shard_map(
        shards,
        mesh=mesh,
        in_specs=(rows, rows, rows, rows, P(("group", "slab")), rows),
        out_specs=rows,
        check_vma=False,
    )
```

time: 100 us -> 52.2 us (0.52)
  the two profiles are of different devices: /device:TPU:1 before, /device:TPU:0 now
where the time goes in v1:
time: 52.2 us; the launch traced here: 52 us
  Pallas kernels  49.5 us (95%)
  local copies, waits for them, and re-layouts  1.87 us (4%)
  between operations  0.66 us (1%)
    pallas_call x1, Pallas kernels, shards(): pl.pallas_call(functools.partial(kernel, groups, slabs), out_shape=jax.Sh...  49.5 us
    unnamed x1, local copies, waits for them, and re-layouts  1.87 us

profile of v1, /device:TPU:0, one launch (start us, length us, event | category | flops | bytes accessed | tf_op | source)
XLA Modules:
  0.0 52.0 jit_solution(12579265491332976593)
XLA Ops:
  0.7 49.5 %shard_map.64 = bf16[512,512]{1,0:T(8,128)(2,1)} custom-call(bf16[512,512]{1,0:T(8,128)(2,1)} %q_ref.1, bf16[512,512]{1,0:T(8,128)(2,1)} %k_ref.1, bf16[512,512]{1,0:T(8,128)(2,1)} %v_ref.1, s32[4,6]{1,0:T(4,128)} %lists_ref.1, s32[1]{0:T(128)S(6)} %copy.8.live_ref, s32[1,4]{1,0:T(1,128)} %ids_ref.1), custom_call_target="tpu_custom_call" | custom-call | tf_op jit(solution)/shard_map/pallas_call | solution.py:227
  50.2 1.9 %copy.9 = bf16[512,512]{1,0:T(8,128)(2,1)} copy(bf16[512,512]{1,0:T(8,128)(2,1)} %shard_map.64) | data formatting | bytes 1048576

commit v2 on v1

--- a/solution.py
+++ b/solution.py
@@ -51,7 +51,7 @@
 
     def slot(place, number):
         if place < 2:
-            return (place * count + number) // 2, lax.rem(place * count + number, 2)
+            return (place * count + number) // 2, (place * count + number) % 2
         return count + number, place - 2
 
     def rows(place, number):
@@ -107,7 +107,7 @@
         for number in range(count):
             for place, first in ((0, 0), (1, near_at), (2, far_at)):
                 chunk, half = slot(place, number)
-                bias[tile, chunk, pl.ds(half, 1)] = jnp.full((1, 2 * TILE), listing(tile, first + number))
+                bias[tile, chunk, :, half * TILE:(half + 1) * TILE] = jnp.full((8, TILE), listing(tile, first + number))
 
     q_copy.wait()
     low = lax.broadcasted_iota(jnp.int32, (TILE, wide), 1) < HEAD_DIM
@@ -120,48 +120,38 @@
     acc[...] = jnp.zeros_like(acc)
     top[...] = jnp.full(top.shape, LOWEST, jnp.float32)
 
-    ones = jnp.ones((16, 2 * TILE), jnp.bfloat16)
-
-    def update(chunk, pair, tile, values):
-        keys = pool_k[chunk, :, pl.ds(pl.multiple_of(pair * wide, wide), wide)]
-        scores = dot(keys, q_pairs[pair, tile], NT)
-        first, second = scores[:TILE], scores[TILE:]
-        first_bias, second_bias = bias[tile, chunk, 0:1], bias[tile, chunk, 1:2]
-        before = top[pair, tile, 0:1]
-        after = jnp.maximum(
-            before,
-            jnp.maximum(
-                jnp.max(first, axis=0, keepdims=True) + first_bias,
-                jnp.max(second, axis=0, keepdims=True) + second_bias,
-            ),
-        )
+    def operands(chunk, pair):
+        at = pl.ds(pl.multiple_of(pair * wide, wide), wide)
+        block = pool_v[chunk, :, at]
+        left = lax.broadcasted_iota(jnp.int32, block.shape, 1) < HEAD_DIM
+        one = jnp.ones_like(block)
+        return pool_k[chunk, :, at], (jnp.where(left, block, one), jnp.where(left, one, block))
+
+    def update(chunk, pair, tile, keys, values):
+        scores = dot(q_pairs[pair, tile], keys, NT) + bias[tile, chunk, 0:1]
+        peak = jnp.max(scores, axis=1, keepdims=True)
+        before = top[pair, tile]
+        after = jnp.maximum(before, peak)
         shrink = jnp.exp2((before - after) * SCALE)
         weights = jnp.concatenate(
             [
-                jnp.exp2((first - (after - first_bias)) * SCALE).astype(jnp.bfloat16),
-                jnp.exp2((second - (after - second_bias)) * SCALE).astype(jnp.bfloat16),
+                jnp.exp2((scores[:, :TILE] - after) * SCALE).astype(jnp.bfloat16),
+                jnp.exp2((scores[:, TILE:] - after) * SCALE).astype(jnp.bfloat16),
             ],
-            axis=0,
+            axis=1,
         )
-        mixed = dot(values, weights, NN)
-        upper = acc[pair, tile, :HEAD_DIM] * shrink + jnp.concatenate(
-            [mixed[:HEAD_DIM, :TILE], mixed[HEAD_DIM:wide, TILE:]], axis=1
-        )
-        total = acc[pair, tile, HEAD_DIM:] * shrink + mixed[wide:wide + 8]
-        return after, upper, total
-
-    def chunk_values(chunk, pair):
-        block = pool_v[chunk, :, pl.ds(pl.multiple_of(pair * wide, wide), wide)]
-        return jnp.concatenate([block.T, ones], axis=0)
+        upper = acc[pair, tile, :TILE] * shrink[:TILE] + dot(weights[:TILE], values[0], NN)
+        lower = acc[pair, tile, TILE:] * shrink[TILE:] + dot(weights[TILE:], values[1], NN)
+        return after, upper, lower
 
     def run(chunk):
         def one_pair(pair, carry):
-            values = chunk_values(chunk, pair)
+            keys, values = operands(chunk, pair)
             for tile in range(count):
-                after, upper, total = update(chunk, pair, tile, values)
-                top[pair, tile, 0:1] = after
-                acc[pair, tile, :HEAD_DIM] = upper
-                acc[pair, tile, HEAD_DIM:] = total
+                after, upper, lower = update(chunk, pair, tile, keys, values)
+                top[pair, tile] = after
+                acc[pair, tile, :TILE] = upper
+                acc[pair, tile, TILE:] = lower
             return carry
 
         lax.fori_loop(0, pairs, one_pair, 0)
@@ -179,11 +169,11 @@
     for tile in range(count):
         given = [listing(tile, 3 * count + entry) for entry in range(count)]
         for number in range(count):
-            row = jnp.full((1, 2 * TILE), NEVER, jnp.float32)
+            row = jnp.full((1, TILE), NEVER, jnp.float32)
             for entry in range(count):
-                hit = jnp.broadcast_to(far_ids[0:1, entry:entry + 1], (1, 2 * TILE)) == number
+                hit = jnp.broadcast_to(far_ids[0:1, entry:entry + 1], (1, TILE)) == number
                 row = jnp.where(hit, given[entry], row)
-            bias[tile, count + number, 1:2] = row
+            bias[tile, count + number, 0:1, TILE:] = row
 
     def later(number, carry):
         for place in (2, 3):
@@ -201,12 +191,12 @@
 
     def last(pair, carry):
         chunk = 2 * count - 1
-        values = chunk_values(chunk, pair)
+        keys, values = operands(chunk, pair)
         for tile in range(count):
-            _, upper, total = update(chunk, pair, tile, values)
-            mixed = upper / total[0:1]
-            mixed = jnp.concatenate([mixed[:, :TILE], mixed[:, TILE:]], axis=0)
-            mixed = jnp.where(tile < live, mixed.T, 0.0)
+            _, upper, lower = update(chunk, pair, tile, keys, values)
+            mixed = jnp.where(low, upper, lower)
+            total = pltpu.roll(jnp.where(low, lower, upper), HEAD_DIM, axis=1)
+            mixed = jnp.where(tile < live, mixed / total, 0.0)
             at = pl.ds(pl.multiple_of(pair * wide, wide), wide)
             out_ref[pl.ds(tile * TILE, TILE), at] = mixed.astype(out_ref.dtype)
         return carry
@@ -234,9 +224,9 @@
                 pltpu.VMEM((2 * count, 2 * TILE, width), values.dtype),
                 pltpu.VMEM((nodes, width), queries.dtype),
                 pltpu.VMEM((pairs, count, 2 * TILE, 2 * HEAD_DIM), queries.dtype),
-                pltpu.VMEM((pairs, count, HEAD_DIM + 8, 2 * TILE), jnp.float32),
-                pltpu.VMEM((pairs, count, 8, 2 * TILE), jnp.float32),
-                pltpu.VMEM((count, 2 * count, 2, 2 * TILE), jnp.float32),
+                pltpu.VMEM((pairs, count, 2 * TILE, 2 * HEAD_DIM), jnp.float32),
+                pltpu.VMEM((pairs, count, 2 * TILE, TILE), jnp.float32),
+                pltpu.VMEM((count, 2 * count, 8, 2 * TILE), jnp.float32),
                 pltpu.VMEM(boundary_ids.shape, jnp.int32),
                 pltpu.SemaphoreType.DMA((3, count)),
                 pltpu.SemaphoreType.DMA((3, 2, count)),

time: 52.2 us -> 38.5 us (0.74)
  Pallas kernels: 49.5 us -> 35.6 us
    pallas_call x1, Pallas kernels: 49.5 us -> 35.6 us  [shards(): pl.pallas_call(functools.partial(kernel, groups, slabs), out_shape=jax.Sh...]
where the time goes in v2:
time: 38.5 us; the launch traced here: 38.1 us
  Pallas kernels  35.6 us (92%)
  local copies, waits for them, and re-layouts  1.87 us (5%)
  between operations  0.66 us (2%)
    pallas_call x1, Pallas kernels, shards(): pl.pallas_call(functools.partial(kernel, groups, slabs), out_shape=jax.Sh...  35.6 us
    unnamed x1, local copies, waits for them, and re-layouts  1.87 us

profile of v2, /device:TPU:0, one launch (start us, length us, event | category | flops | bytes accessed | tf_op | source)
XLA Modules:
  0.0 38.1 jit_solution(10311444703213760743)
XLA Ops:
  0.7 35.6 %shard_map.64 = bf16[512,512]{1,0:T(8,128)(2,1)} custom-call(bf16[512,512]{1,0:T(8,128)(2,1)} %q_ref.1, bf16[512,512]{1,0:T(8,128)(2,1)} %k_ref.1, bf16[512,512]{1,0:T(8,128)(2,1)} %v_ref.1, s32[4,6]{1,0:T(4,128)} %lists_ref.1, s32[1]{0:T(128)S(6)} %copy.8.live_ref, s32[1,4]{1,0:T(1,128)} %ids_ref.1), custom_call_target="tpu_custom_call" | custom-call | tf_op jit(solution)/shard_map/pallas_call | solution.py:217
  36.2 1.9 %copy.9 = bf16[512,512]{1,0:T(8,128)(2,1)} copy(bf16[512,512]{1,0:T(8,128)(2,1)} %shard_map.64) | data formatting | bytes 1048576

commit v3 on v2

v3 whole, which is shorter than its diff:
```python
import functools
import math

import jax
import jax.numpy as jnp
from jax import lax
from jax.experimental import pallas as pl
from jax.experimental.pallas import tpu as pltpu
from jax.sharding import PartitionSpec as P

HEAD_DIM = 64
TILE = 128
SCALE = HEAD_DIM ** (-0.5) * math.log2(math.e)
NT = (((1,), (1,)), ((), ()))
NN = (((1,), (0,)), ((), ()))


def dot(a, b, dims):
    return lax.dot_general(a, b, dims, preferred_element_type=jnp.float32)


def kernel(
    groups, slabs,
    q_ref, k_ref, v_ref, lists_ref, live_ref, ids_ref,
    out_ref,
    pool_k, pool_v, q_raw, q_pairs, weights, far_ids, near_ids,
    local_sem, send_sem, recv_sem, ids_sem,
):
    count = lists_ref.shape[0]
    listed = lists_ref.shape[1]
    pairs = q_pairs.shape[0]
    wide = 2 * HEAD_DIM
    group = lax.axis_index("group")
    slab = lax.axis_index("slab")
    odd = lax.rem(slab, 2)
    near = slab + 1 - 2 * odd
    far = lax.rem(slab - 1 + 2 * odd + slabs, slabs)
    ahead = lax.rem(group + 1, groups)
    behind = lax.rem(group - 1 + groups, groups)
    at_near = {"group": group, "slab": near}
    at_far = {"group": group, "slab": far}
    at_ahead = {"group": ahead, "slab": slab}
    at_behind = {"group": behind, "slab": slab}
    mesh_id = pl.DeviceIdType.MESH

    barrier = pltpu.get_barrier_semaphore()
    for device in (at_near, at_far, at_behind):
        pl.semaphore_signal(barrier, inc=1, device_id=device, device_id_type=mesh_id)

    sources = ((k_ref, pool_k), (v_ref, pool_v))

    def own(kind):
        ref, pool = sources[kind]
        return pltpu.make_async_copy(ref, pool.at[pl.ds(0, count)], local_sem.at[kind])

    def remote(place, kind):
        ref, pool = sources[kind]
        return pltpu.make_async_remote_copy(
            src_ref=ref,
            dst_ref=pool.at[pl.ds(place * count, count)],
            send_sem=send_sem.at[place - 1, kind],
            recv_sem=recv_sem.at[place - 1, kind],
            device_id=(at_near, at_far, at_ahead)[place - 1],
            device_id_type=mesh_id,
        )

    q_copy = pltpu.make_async_copy(q_ref, q_raw, local_sem.at[2])
    q_copy.start()
    own(0).start()
    own(1).start()
    ids_copy = pltpu.make_async_remote_copy(
        src_ref=ids_ref, dst_ref=far_ids, send_sem=ids_sem.at[0], recv_sem=ids_sem.at[1],
        device_id=at_ahead, device_id_type=mesh_id,
    )
    pl.semaphore_wait(barrier, 3)
    ids_copy.start()
    for kind in range(2):
        for place in (3, 2, 1):
            remote(place, kind).start()

    q_copy.wait()
    low = lax.broadcasted_iota(jnp.int32, (TILE, wide), 1) < HEAD_DIM
    for pair in range(pairs):
        for tile in range(count):
            block = q_raw[pl.ds(tile * TILE, TILE), pl.ds(pair * wide, wide)]
            zero = jnp.zeros_like(block)
            q_pairs[pair, tile, pl.ds(0, TILE)] = jnp.where(low, block, zero)
            q_pairs[pair, tile, pl.ds(TILE, TILE)] = jnp.where(low, zero, block)

    ids_copy.wait()
    ids_local = pltpu.make_async_copy(far_ids, near_ids, local_sem.at[3])
    ids_local.start()
    ids_local.wait()
    swap = count * (1 - odd)

    def slot(tile, entry):
        place = lists_ref[tile, entry]
        found = jnp.where(place < 2 * count, place + swap, place - swap)
        found = jnp.where(place < count, place, found)
        for number in range(count):
            found = jnp.where(place == 3 * count + number, 3 * count + near_ids[0, number], found)
        return found

    def gathered(pool, tile, at):
        return jnp.concatenate([pool[slot(tile, entry), :, at] for entry in range(listed)], axis=0)

    live = live_ref[0]

    def weigh(pair, carry):
        at = pl.ds(pl.multiple_of(pair * wide, wide), wide)
        for tile in range(count):
            scores = dot(q_pairs[pair, tile], gathered(pool_k, tile, at), NT)
            peak = jnp.max(scores, axis=1, keepdims=True)
            raised = jnp.exp2((scores - peak) * SCALE)
            total = jnp.sum(raised, axis=1, keepdims=True)
            share = jnp.where(tile < live, 1.0 / total, 0.0)
            weights[pair, tile] = (raised * share).astype(jnp.bfloat16)
        return carry

    def mix(pair, carry):
        at = pl.ds(pl.multiple_of(pair * wide, wide), wide)
        for tile in range(count):
            mixed = dot(weights[pair, tile], gathered(pool_v, tile, at), NN)
            mixed = jnp.where(low, mixed[:TILE], mixed[TILE:])
            out_ref[pl.ds(tile * TILE, TILE), at] = mixed.astype(out_ref.dtype)
        return carry

    for kind, step in ((0, weigh), (1, mix)):
        own(kind).wait()
        for place in (1, 2, 3):
            remote(place, kind).wait()
        lax.fori_loop(0, pairs, step, 0)


def solution(mesh):
    groups, slabs = mesh.shape["group"], mesh.shape["slab"]

    def shards(queries, keys, values, neighbours, live_tiles, boundary_ids):
        nodes, width = queries.shape
        count = neighbours.shape[0]
        pairs = width // (2 * HEAD_DIM)
        anywhere = pl.BlockSpec(memory_space=pl.ANY)
        scalars = pl.BlockSpec(memory_space=pltpu.SMEM)
        inside = pl.BlockSpec(memory_space=pltpu.VMEM)
        return pl.pallas_call(
            functools.partial(kernel, groups, slabs),
            out_shape=jax.ShapeDtypeStruct((nodes, width), queries.dtype),
            in_specs=[anywhere, anywhere, anywhere, scalars, scalars, inside],
            out_specs=inside,
            scratch_shapes=[
                pltpu.VMEM((4 * count, TILE, width), keys.dtype),
                pltpu.VMEM((4 * count, TILE, width), values.dtype),
                pltpu.VMEM((nodes, width), queries.dtype),
                pltpu.VMEM((pairs, count, 2 * TILE, 2 * HEAD_DIM), queries.dtype),
                pltpu.VMEM((pairs, count, 2 * TILE, neighbours.shape[1] * TILE), jnp.bfloat16),
                pltpu.VMEM(boundary_ids.shape, jnp.int32),
                pltpu.SMEM(boundary_ids.shape, jnp.int32),
                pltpu.SemaphoreType.DMA((4,)),
                pltpu.SemaphoreType.DMA((3, 2)),
                pltpu.SemaphoreType.DMA((3, 2)),
                pltpu.SemaphoreType.DMA((2,)),
            ],
            compiler_params=pltpu.CompilerParams(collective_id=0, has_side_effects=True),
        )(queries, keys.reshape(count, TILE, width), values.reshape(count, TILE, width), neighbours, live_tiles, boundary_ids)

    rows = P(("group", "slab"), None)
    return jax.shard_map(
        shards,
        mesh=mesh,
        in_specs=(rows, rows, rows, rows, P(("group", "slab")), rows),
        out_specs=rows,
        check_vma=False,
    )
```

time: 38.5 us -> 34.9 us (0.906)
  Pallas kernels: 35.6 us -> 32.2 us
    pallas_call x1, Pallas kernels: 35.6 us -> 32.2 us  [shards(): pl.pallas_call(functools.partial(kernel, groups, slabs), out_shape=jax.Sh...]
where the time goes in v3:
time: 34.9 us; the launch traced here: 34.7 us
  Pallas kernels  32.2 us (92%)
  local copies, waits for them, and re-layouts  1.87 us (5%)
  between operations  0.66 us (2%)
    pallas_call x1, Pallas kernels, shards(): pl.pallas_call(functools.partial(kernel, groups, slabs), out_shape=jax.Sh...  32.2 us
    unnamed x1, local copies, waits for them, and re-layouts  1.87 us

profile of v3, /device:TPU:0, one launch (start us, length us, event | category | flops | bytes accessed | tf_op | source)
XLA Modules:
  0.0 34.7 jit_solution(3032326087685412848)
XLA Ops:
  0.7 32.2 %shard_map.64 = bf16[512,512]{1,0:T(8,128)(2,1)} custom-call(bf16[512,512]{1,0:T(8,128)(2,1)} %q_ref.1, bf16[4,128,512]{2,1,0:T(8,128)(2,1)} %bitcast.2, bf16[4,128,512]{2,1,0:T(8,128)(2,1)} %bitcast.3, s32[4,6]{1,0:T(4,128)} %lists_ref.1, s32[1]{0:T(128)S(6)} %copy.8.live_ref, s32[1,4]{1,0:T(1,128)} %ids_ref.1), custom_call_target="tpu_custom_call" | custom-call | tf_op jit(solution)/shard_map/pallas_call | solution.py:145
  32.9 1.9 %copy.9 = bf16[512,512]{1,0:T(8,128)(2,1)} copy(bf16[512,512]{1,0:T(8,128)(2,1)} %shard_map.64) | data formatting | bytes 1048576

commit v4 on v3

--- a/solution.py
+++ b/solution.py
@@ -107,7 +107,7 @@
     live = live_ref[0]
 
     def weigh(pair, carry):
-        at = pl.ds(pl.multiple_of(pair * wide, wide), wide)
+        at = pl.ds(pair * wide, wide)
         for tile in range(count):
             scores = dot(q_pairs[pair, tile], gathered(pool_k, tile, at), NT)
             peak = jnp.max(scores, axis=1, keepdims=True)
@@ -118,7 +118,7 @@
         return carry
 
     def mix(pair, carry):
-        at = pl.ds(pl.multiple_of(pair * wide, wide), wide)
+        at = pl.ds(pair * wide, wide)
         for tile in range(count):
             mixed = dot(weights[pair, tile], gathered(pool_v, tile, at), NN)
             mixed = jnp.where(low, mixed[:TILE], mixed[TILE:])
@@ -129,7 +129,8 @@
         own(kind).wait()
         for place in (1, 2, 3):
             remote(place, kind).wait()
-        lax.fori_loop(0, pairs, step, 0)
+        for pair in range(pairs):
+            step(pair, 0)
 
 
 def solution(mesh):

time: 34.9 us -> 34.4 us (0.986)
  Pallas kernels: 32.2 us -> 31.6 us
    pallas_call x1, Pallas kernels: 32.2 us -> 31.6 us  [shards(): pl.pallas_call(functools.partial(kernel, groups, slabs), out_shape=jax.Sh...]
where the time goes in v4:
time: 34.4 us; the launch traced here: 34.2 us
  Pallas kernels  31.6 us (92%)
  local copies, waits for them, and re-layouts  1.87 us (5%)
  between operations  0.66 us (2%)
    pallas_call x1, Pallas kernels, shards(): pl.pallas_call(functools.partial(kernel, groups, slabs), out_shape=jax.Sh...  31.6 us
    unnamed x1, local copies, waits for them, and re-layouts  1.87 us

profile of v4, /device:TPU:0, one launch (start us, length us, event | category | flops | bytes accessed | tf_op | source)
XLA Modules:
  0.0 34.2 jit_solution(14635775344046026862)
XLA Ops:
  0.7 31.6 %shard_map.64 = bf16[512,512]{1,0:T(8,128)(2,1)} custom-call(bf16[512,512]{1,0:T(8,128)(2,1)} %q_ref.1, bf16[4,128,512]{2,1,0:T(8,128)(2,1)} %bitcast.2, bf16[4,128,512]{2,1,0:T(8,128)(2,1)} %bitcast.3, s32[4,6]{1,0:T(4,128)} %lists_ref.1, s32[1]{0:T(128)S(6)} %copy.8.live_ref, s32[1,4]{1,0:T(1,128)} %ids_ref.1), custom_call_target="tpu_custom_call" | custom-call | tf_op jit(solution)/shard_map/pallas_call | solution.py:146
  32.3 1.9 %copy.9 = bf16[512,512]{1,0:T(8,128)(2,1)} copy(bf16[512,512]{1,0:T(8,128)(2,1)} %shard_map.64) | data formatting | bytes 1048576
